TPU v7x, 256 devices: a whole 4x4x8 slice. The times are simulated.
256 devices in a mesh: slot: 8 (over y, core), asset: 32 (over x, z).
Axes of the slice: x: 4, y: 4, z: 8, core: 2. Of those that a mesh axis runs over, the one named last changes fastest.
Arguments:
- slot_emb: bfloat16 [16384, 768], P(('slot', 'asset')), may hold values from -4 to 4
- asset_panel: bfloat16 [768, 32768], P('slot', 'asset'), may hold values from -4 to 4
- mult: int32 [16384], P('slot'), may hold values from 1 to 4
- caps: int32 [32768], P('asset'), may hold values from 1 to 8, as said below
Outputs:
- plan: float32 [16384, 32768], P('slot', 'asset')
Inputs may be any that keep to these rules, and one draw needn't show every extreme that they name: caps are whole numbers; the last asset's cap is the largest.
All inputs are finite; a program needn't handle non-finite values.
Results may differ from a plain program's by a relative error of at most 0.0003.
Values may be sent and summed in bfloat16 or wider, within the bound.
No kernel may reach another device: no remote copies, remote signals or barrier semaphores. Data moves between devices by JAX's collectives and lax.ppermute only.
A program may use at most 64 MiB of HBM per device.

v0:
```python
import jax
import jax.numpy as jnp
from jax import lax
from jax.sharding import PartitionSpec as P

EMB = 768
ITERS = 3


def row_side(logits, asset_pot):
    shifted = logits + asset_pot[None, :]
    peak = lax.pmax(jnp.max(shifted, axis=1), "asset")
    total = lax.psum(jnp.sum(jnp.exp(shifted - peak[:, None]), axis=1), "asset")
    return peak + jnp.log(total)


def col_side(logits, slot_pot):
    shifted = logits + slot_pot[:, None]
    peak = lax.pmax(jnp.max(shifted, axis=0), "slot")
    total = lax.psum(jnp.sum(jnp.exp(shifted - peak[None, :]), axis=0), "slot")
    return peak + jnp.log(total)


def per_device(slot_emb, asset_panel, mult, caps):
    slot_block = lax.all_gather(slot_emb, "asset", axis=0, tiled=True)
    logits = jnp.dot(
        slot_block,
        lax.all_gather(asset_panel, "slot", axis=0, tiled=True),
        preferred_element_type=jnp.float32,
    ) * EMB ** (-0.5)
    caps_float = caps.astype(jnp.float32)
    cap_total = lax.psum(jnp.sum(caps_float), "asset")
    log_b = jnp.log(caps_float) - jnp.log(cap_total)
    log_a = jnp.log(mult.astype(jnp.float32))
    asset_pot = jnp.zeros((logits.shape[1],), jnp.float32)
    slot_pot = jnp.zeros((logits.shape[0],), jnp.float32)
    for iteration in range(ITERS):
        slot_pot = log_a - row_side(logits, asset_pot)
        asset_pot = log_b - col_side(logits, slot_pot)
    factor = float(
        logits.shape[0] * lax.axis_size("slot") * logits.shape[1] * lax.axis_size("asset")
    )
    return jnp.exp(logits + slot_pot[:, None] + asset_pot[None, :]) * factor


def solution(mesh):
    return jax.shard_map(
        per_device,
        mesh=mesh,
        in_specs=(P(("slot", "asset"), None), P("slot", "asset"), P("slot"), P("asset")),
        out_specs=P("slot", "asset"),
        check_vma=False,
    )
```

profile of v0, /device:TPU:1, one launch (start us, length us, event | category | flops | bytes accessed | tf_op | source)
XLA Modules:
  0.0 697.3 jit_solution(16595806168147780768)
XLA Ops:
  6.5 0.0 all-gather.5.cloned.1.call-start
  6.5 0.7 all-gather.5.cloned.1.call-update
  7.3 0.0 all-gather.3.cloned.1.call-start
  7.3 0.7 all-gather.3.cloned.1.call-update
  8.0 1.3 convert_reduce_fusion
  9.3 31.0 %all-gather.5.cloned.1.call-done = bf16[768,1024]{1,0:T(8,128)(2,1)} async-done(((bf16[96,1024]{1,0:T(8,128)(2,1)}), bf16[768,1024]{1,0:T(8,128)(2,1)}) %all-gather.5.cloned.1.call-update) | async-done | bytes 1572880 | tf_op jit(solution)/shard_map/all_gather | solution.py:28
  40.3 77.9 %all-gather.3.cloned.1.call-done = bf16[2048,768]{1,0:T(8,128)(2,1)} async-done(((bf16[64,768]{1,0:T(8,128)(2,1)}), bf16[2048,768]{1,0:T(8,128)(2,1)}) %all-gather.3.cloned.1.call-update) | async-done | bytes 3145744 | tf_op jit(solution)/shard_map/all_gather | solution.py:25
  118.2 9.2 %fusion = (f32[2048]{0:T(1024)S(1)}, f32[2048,1024]{1,0:T(8,128)}) fusion(bf16[2048,768]{1,0:T(8,128)(2,1)} %all-gather.3.cloned.1.call-done, bf16[768,1024]{1,0:T(8,128)(2,1)} %all-gather.5.cloned.1.call-done), kind=kOutput, calls=%fused_computation.22 | convolution fusion | flops 3225417728 | bytes 13115392 | tf_op jit(solution)/shard_map/dot_general | solution.py:26
  127.4 0.0 copy-start
  127.4 58.9 %pmax.42 = f32[2048]{0:T(1024)S(1)} all-reduce(f32[2048]{0:T(1024)S(1)} %get-tuple-element.7), channel_id=1, replica_groups=mesh['slot'=8,'asset'=32] {'asset'}, use_global_device_ids=true, to_apply=%region_3.0 | all-reduce | flops 2048 | bytes 16384 | tf_op jit(solution)/shard_map/pmax | solution.py:12
  186.3 4.4 exponential_reduce_fusion.5
  190.7 58.3 %all-reduce = (f32[2048]{0:T(1024)S(1)}, f32[]{:T(128)}) all-reduce(f32[2048]{0:T(1024)S(1)} %exponential_reduce_fusion.5, f32[]{:T(128)} %convert_reduce_fusion), channel_id=1, replica_groups=mesh['slot'=8,'asset'=32] {'asset'}, use_global_device_ids=true, to_apply=%region_5.0 | all-reduce | flops 2049 | bytes 16392 | tf_op jit(solution)/shard_map/psum | solution.py:13
  249.6 0.0 copy-done
  249.6 0.0 copy-start.1
  249.6 4.0 add_reduce_fusion.3
  253.6 44.0 %pmax.43 = f32[1024]{0:T(1024)S(1)} all-reduce(f32[1024]{0:T(1024)S(1)} %add_reduce_fusion.3), channel_id=1, replica_groups=mesh['slot'=8,'asset'=32] {'slot'}, use_global_device_ids=true, to_apply=%region_7.0 | all-reduce | flops 1024 | bytes 8192 | tf_op jit(solution)/shard_map/pmax | solution.py:19
  297.6 4.2 exponential_reduce_fusion.4
  301.9 12.4 %psum.51 = f32[1024]{0:T(1024)S(1)} all-reduce(f32[1024]{0:T(1024)S(1)} %exponential_reduce_fusion.4), channel_id=1, replica_groups=mesh['slot'=8,'asset'=32] {'slot'}, use_global_device_ids=true, to_apply=%region_9.0 | all-reduce | flops 1024 | bytes 8192 | tf_op jit(solution)/shard_map/psum | solution.py:20
  314.3 0.0 copy-done.1
  314.3 4.0 add_reduce_fusion.2
  318.3 59.1 %pmax.44 = f32[2048]{0:T(1024)S(1)} all-reduce(f32[2048]{0:T(1024)S(1)} %add_reduce_fusion.2), channel_id=1, replica_groups=mesh['slot'=8,'asset'=32] {'asset'}, use_global_device_ids=true, to_apply=%region_11.0 | all-reduce | flops 2048 | bytes 16384 | tf_op jit(solution)/shard_map/pmax | solution.py:12
  377.5 4.4 exponential_reduce_fusion.3
  381.8 57.1 %psum.52 = f32[2048]{0:T(1024)S(1)} all-reduce(f32[2048]{0:T(1024)S(1)} %exponential_reduce_fusion.3), channel_id=1, replica_groups=mesh['slot'=8,'asset'=32] {'asset'}, use_global_device_ids=true, to_apply=%region_13.0 | all-reduce | flops 2048 | bytes 16384 | tf_op jit(solution)/shard_map/psum | solution.py:13
  438.9 4.0 add_reduce_fusion.1
  442.9 39.6 %pmax.45 = f32[1024]{0:T(1024)S(1)} all-reduce(f32[1024]{0:T(1024)S(1)} %add_reduce_fusion.1), channel_id=1, replica_groups=mesh['slot'=8,'asset'=32] {'slot'}, use_global_device_ids=true, to_apply=%region_15.0 | all-reduce | flops 1024 | bytes 8192 | tf_op jit(solution)/shard_map/pmax | solution.py:19
  482.5 4.2 exponential_reduce_fusion.2
  486.8 12.4 %psum.53 = f32[1024]{0:T(1024)S(1)} all-reduce(f32[1024]{0:T(1024)S(1)} %exponential_reduce_fusion.2), channel_id=1, replica_groups=mesh['slot'=8,'asset'=32] {'slot'}, use_global_device_ids=true, to_apply=%region_17.0 | all-reduce | flops 1024 | bytes 8192 | tf_op jit(solution)/shard_map/psum | solution.py:20
  499.2 4.0 add_reduce_fusion
  503.2 59.2 %pmax.46 = f32[2048]{0:T(1024)S(1)} all-reduce(f32[2048]{0:T(1024)S(1)} %add_reduce_fusion), channel_id=1, replica_groups=mesh['slot'=8,'asset'=32] {'asset'}, use_global_device_ids=true, to_apply=%region_19.0 | all-reduce | flops 2048 | bytes 16384 | tf_op jit(solution)/shard_map/pmax | solution.py:12
  562.4 4.4 exponential_reduce_fusion.1
  566.7 57.0 %psum.54 = f32[2048]{0:T(1024)S(1)} all-reduce(f32[2048]{0:T(1024)S(1)} %exponential_reduce_fusion.1), channel_id=1, replica_groups=mesh['slot'=8,'asset'=32] {'asset'}, use_global_device_ids=true, to_apply=%region_21.0 | all-reduce | flops 2048 | bytes 16384 | tf_op jit(solution)/shard_map/psum | solution.py:13
  623.8 4.0 add_reduce_fusion.4
  627.8 39.6 %pmax.47 = f32[1024]{0:T(1024)S(1)} all-reduce(f32[1024]{0:T(1024)S(1)} %add_reduce_fusion.4), channel_id=1, replica_groups=mesh['slot'=8,'asset'=32] {'slot'}, use_global_device_ids=true, to_apply=%region_23.0 | all-reduce | flops 1024 | bytes 8192 | tf_op jit(solution)/shard_map/pmax | solution.py:19
  667.4 4.2 exponential_reduce_fusion
  671.7 12.4 %psum.55 = f32[1024]{0:T(1024)S(1)} all-reduce(f32[1024]{0:T(1024)S(1)} %exponential_reduce_fusion), channel_id=1, replica_groups=mesh['slot'=8,'asset'=32] {'slot'}, use_global_device_ids=true, to_apply=%region_25.0 | all-reduce | flops 1024 | bytes 8192 | tf_op jit(solution)/shard_map/psum | solution.py:20
  684.1 6.3 exponential_multiply_fusion
  (6 shorter events, 0.1 us)
Async XLA Ops:
  6.5 33.7 %all-gather.5.cloned.1.call-start = ((), (), s32[]{:S(2)}) async-start(), calls=%async_computation.1 | async-start | bytes 1769472 | tf_op jit(solution)/shard_map/all_gather | solution.py:28
  7.3 110.9 %all-gather.3.cloned.1.call-start = ((), (), s32[]{:S(2)}) async-start(), calls=%async_computation | async-start | bytes 3244032 | tf_op jit(solution)/shard_map/all_gather | solution.py:25
  127.4 122.2 %copy-start = (s32[2048]{0:T(1024)S(1)}, s32[2048]{0:T(1024)}, u32[]{:S(2)}) copy-start(s32[2048]{0:T(1024)} %param.6) | copy-start | bytes 24580
  249.6 64.7 %copy-start.1 = (s32[1024]{0:T(1024)S(1)}, s32[1024]{0:T(1024)}, u32[]{:S(2)}) copy-start(s32[1024]{0:T(1024)} %param.7) | copy-start | bytes 12292
Sparse Core Ops, SparseCore 0:
  9.2 31.0 all-gather.4
  42.8 75.2 all-gather.2
where the time goes:
time: 698 us; the launch traced here: 697 us
  blocking collectives  510 us (73%)
  waiting for transfers between devices  110 us (16%)
  other arithmetic  53.5 us (8%)
  between operations  14.2 us (2%)
  matrix products  9.19 us (1%)
    pmax x3, blocking collectives, row_side(): peak = lax.pmax(jnp.max(shifted, axis=1), 'asset')  177 us
    psum x3, blocking collectives, row_side(): total = lax.psum(jnp.sum(jnp.exp(shifted - peak[:, None]), axis=1), 'asset')  172 us
    pmax x3, blocking collectives, col_side(): peak = lax.pmax(jnp.max(shifted, axis=0), 'slot')  123 us
    all_gather x1, waiting for transfers between devices, per_device(): slot_block = lax.all_gather(slot_emb, 'asset', axis=0, tiled=True)  77.9 us
    psum x3, blocking collectives, col_side(): total = lax.psum(jnp.sum(jnp.exp(shifted - peak[None, :]), axis=0), 'slot')  37.3 us
    all_gather x1, waiting for transfers between devices, per_device(): lax.all_gather(asset_panel, 'slot', axis=0, tiled=True)  31 us
  transfers between devices with their start and end apart: 2, of which 2 were waited for; matrix products, arithmetic and copies ran while one was open for 0% of the time, Pallas kernels for 0%

commit v1 on v0

--- a/solution.py
+++ b/solution.py
@@ -22,7 +22,12 @@
 
 
 def per_device(slot_emb, asset_panel, mult, caps):
-    slot_block = lax.all_gather(slot_emb, "asset", axis=0, tiled=True)
+    slot_block = jnp.concatenate(
+        jax.lax.all_to_all(
+            jnp.stack([slot_emb for _ in range(jax.lax.psum(1, "asset"))], 0), "asset", 0, 0
+        ),
+        0,
+    )
     logits = jnp.dot(
         slot_block,
         lax.all_gather(asset_panel, "slot", axis=0, tiled=True),

time: 698 us -> 670 us (0.960)
  waiting for transfers between devices: 110 us -> 70.9 us
  starting transfers between devices: 0.04 us -> 11.9 us
    all_gather x1 -> x0, waiting for transfers between devices: 77.9 us -> none  [per_device(): slot_block = lax.all_gather(slot_emb, 'asset', axis=0, tiled=True)]
    all_to_all x0 -> x1, waiting for transfers between devices: none -> 39.8 us  [per_device(): jax.lax.all_to_all(jnp.stack([slot_emb for _ in range(jax.lax.psum(1, 'as...]
    all_to_all x0 -> x1, starting transfers between devices: none -> 11.9 us  [per_device(): jax.lax.all_to_all(jnp.stack([slot_emb for _ in range(jax.lax.psum(1, 'as...]
where the time goes in v1:
time: 670 us
  blocking collectives  510 us (76%)
  waiting for transfers between devices  70.9 us (11%)
  other arithmetic  52.9 us (8%)
  between operations  14.2 us (2%)
  starting transfers between devices  11.9 us (2%)
  matrix products  7.11 us (1%)
    pmax x3, blocking collectives, row_side(): peak = lax.pmax(jnp.max(shifted, axis=1), 'asset')  177 us
    psum x3, blocking collectives, row_side(): total = lax.psum(jnp.sum(jnp.exp(shifted - peak[:, None]), axis=1), 'asset')  174 us
    pmax x3, blocking collectives, col_side(): peak = lax.pmax(jnp.max(shifted, axis=0), 'slot')  122 us
    all_to_all x1, waiting for transfers between devices, per_device(): jax.lax.all_to_all(jnp.stack([slot_emb for _ in range(jax.lax.psum(1, 'as...  39.8 us
    psum x3, blocking collectives, col_side(): total = lax.psum(jnp.sum(jnp.exp(shifted - peak[None, :]), axis=0), 'slot')  37.1 us
    all_gather x1, waiting for transfers between devices, per_device(): lax.all_gather(asset_panel, 'slot', axis=0, tiled=True)  30.3 us
  transfers between devices with their start and end apart: 2, of which 2 were waited for; matrix products, arithmetic and copies ran while one was open for 0% of the time, Pallas kernels for 0%

profile of v1, /device:TPU:1, one launch (start us, length us, event | category | flops | bytes accessed | tf_op | source)
XLA Modules:
  0.0 669.5 jit_solution(4915027837957662886)
XLA Ops:
  6.5 0.0 copy-start.1
  6.5 2.9 stack.2
  9.5 11.9 %all-to-all-start = ((bf16[32,64,768]{2,1,0:T(8,128)(2,1)}), bf16[32,64,768]{2,1,0:T(8,128)(2,1)S(1)}, u32[]{:S(2)}, u32[]{:S(2)}) async-start(bf16[32,64,768]{2,1,0:T(8,128)(2,1)} %stack.2), calls=%async_computation | async-start | bytes 6291456 | tf_op jit(solution)/shard_map/all_to_all | solution.py:26
  21.3 0.0 all-gather.2.cloned.1.call-start
  21.4 0.7 all-gather.2.cloned.1.call-update
  22.1 0.0 copy-done.1
  22.1 0.6 convert_reduce_fusion
  22.7 30.3 %all-gather.2.cloned.1.call-done = bf16[768,1024]{1,0:T(8,128)(2,1)} async-done(((bf16[96,1024]{1,0:T(8,128)(2,1)}), bf16[768,1024]{1,0:T(8,128)(2,1)}) %all-gather.2.cloned.1.call-update) | async-done | bytes 1572880 | tf_op jit(solution)/shard_map/all_gather | solution.py:33
  53.1 39.8 %all-to-all-done = bf16[32,64,768]{2,1,0:T(8,128)(2,1)S(1)} async-done(((bf16[32,64,768]{2,1,0:T(8,128)(2,1)}), bf16[32,64,768]{2,1,0:T(8,128)(2,1)S(1)}, u32[]{:S(2)}, u32[]{:S(2)}) %all-to-all-start) | async-done | bytes 3145760 | tf_op jit(solution)/shard_map/all_to_all | solution.py:26
  92.9 7.1 %fusion = (f32[2048]{0:T(1024)S(1)}, f32[2048,1024]{1,0:T(8,128)}) fusion(bf16[2048,768]{1,0:T(8,128)(2,1)S(1)} %bitcast.3, bf16[768,1024]{1,0:T(8,128)(2,1)} %all-gather.2.cloned.1.call-done), kind=kOutput, calls=%fused_computation.22 | convolution fusion | flops 3225417728 | bytes 13115392 | tf_op jit(solution)/shard_map/dot_general | solution.py:31
  100.0 0.0 copy-start
  100.0 60.6 %pmax.42 = f32[2048]{0:T(1024)S(1)} all-reduce(f32[2048]{0:T(1024)S(1)} %get-tuple-element.7), channel_id=1, replica_groups=mesh['slot'=8,'asset'=32] {'asset'}, use_global_device_ids=true, to_apply=%region_3.0 | all-reduce | flops 2048 | bytes 16384 | tf_op jit(solution)/shard_map/pmax | solution.py:12
  160.6 4.4 exponential_reduce_fusion.5
  165.0 58.8 %all-reduce = (f32[2048]{0:T(1024)S(1)}, f32[]{:T(128)}) all-reduce(f32[2048]{0:T(1024)S(1)} %exponential_reduce_fusion.5, f32[]{:T(128)} %convert_reduce_fusion), channel_id=1, replica_groups=mesh['slot'=8,'asset'=32] {'asset'}, use_global_device_ids=true, to_apply=%region_5.0 | all-reduce | flops 2049 | bytes 16392 | tf_op jit(solution)/shard_map/psum | solution.py:13
  224.5 0.0 copy-done
  224.5 4.0 add_reduce_fusion.3
  228.5 41.5 %pmax.43 = f32[1024]{0:T(1024)S(1)} all-reduce(f32[1024]{0:T(1024)S(1)} %add_reduce_fusion.3), channel_id=1, replica_groups=mesh['slot'=8,'asset'=32] {'slot'}, use_global_device_ids=true, to_apply=%region_7.0 | all-reduce | flops 1024 | bytes 8192 | tf_op jit(solution)/shard_map/pmax | solution.py:19
  270.0 4.2 exponential_reduce_fusion.4
  274.2 12.3 %psum.51 = f32[1024]{0:T(1024)S(1)} all-reduce(f32[1024]{0:T(1024)S(1)} %exponential_reduce_fusion.4), channel_id=1, replica_groups=mesh['slot'=8,'asset'=32] {'slot'}, use_global_device_ids=true, to_apply=%region_9.0 | all-reduce | flops 1024 | bytes 8192 | tf_op jit(solution)/shard_map/psum | solution.py:20
  286.5 4.0 add_reduce_fusion.2
  290.5 58.1 %pmax.44 = f32[2048]{0:T(1024)S(1)} all-reduce(f32[2048]{0:T(1024)S(1)} %add_reduce_fusion.2), channel_id=1, replica_groups=mesh['slot'=8,'asset'=32] {'asset'}, use_global_device_ids=true, to_apply=%region_11.0 | all-reduce | flops 2048 | bytes 16384 | tf_op jit(solution)/shard_map/pmax | solution.py:12
  348.7 4.4 exponential_reduce_fusion.3
  353.1 57.6 %psum.52 = f32[2048]{0:T(1024)S(1)} all-reduce(f32[2048]{0:T(1024)S(1)} %exponential_reduce_fusion.3), channel_id=1, replica_groups=mesh['slot'=8,'asset'=32] {'asset'}, use_global_device_ids=true, to_apply=%region_13.0 | all-reduce | flops 2048 | bytes 16384 | tf_op jit(solution)/shard_map/psum | solution.py:13
  410.6 4.0 add_reduce_fusion.1
  414.7 40.1 %pmax.45 = f32[1024]{0:T(1024)S(1)} all-reduce(f32[1024]{0:T(1024)S(1)} %add_reduce_fusion.1), channel_id=1, replica_groups=mesh['slot'=8,'asset'=32] {'slot'}, use_global_device_ids=true, to_apply=%region_15.0 | all-reduce | flops 1024 | bytes 8192 | tf_op jit(solution)/shard_map/pmax | solution.py:19
  454.8 4.2 exponential_reduce_fusion.2
  459.0 12.4 %psum.53 = f32[1024]{0:T(1024)S(1)} all-reduce(f32[1024]{0:T(1024)S(1)} %exponential_reduce_fusion.2), channel_id=1, replica_groups=mesh['slot'=8,'asset'=32] {'slot'}, use_global_device_ids=true, to_apply=%region_17.0 | all-reduce | flops 1024 | bytes 8192 | tf_op jit(solution)/shard_map/psum | solution.py:20
  471.4 4.0 add_reduce_fusion
  475.5 58.1 %pmax.46 = f32[2048]{0:T(1024)S(1)} all-reduce(f32[2048]{0:T(1024)S(1)} %add_reduce_fusion), channel_id=1, replica_groups=mesh['slot'=8,'asset'=32] {'asset'}, use_global_device_ids=true, to_apply=%region_19.0 | all-reduce | flops 2048 | bytes 16384 | tf_op jit(solution)/shard_map/pmax | solution.py:12
  533.6 4.4 exponential_reduce_fusion.1
  537.9 57.6 %psum.54 = f32[2048]{0:T(1024)S(1)} all-reduce(f32[2048]{0:T(1024)S(1)} %exponential_reduce_fusion.1), channel_id=1, replica_groups=mesh['slot'=8,'asset'=32] {'asset'}, use_global_device_ids=true, to_apply=%region_21.0 | all-reduce | flops 2048 | bytes 16384 | tf_op jit(solution)/shard_map/psum | solution.py:13
  595.6 4.0 add_reduce_fusion.4
  599.6 40.1 %pmax.47 = f32[1024]{0:T(1024)S(1)} all-reduce(f32[1024]{0:T(1024)S(1)} %add_reduce_fusion.4), channel_id=1, replica_groups=mesh['slot'=8,'asset'=32] {'slot'}, use_global_device_ids=true, to_apply=%region_23.0 | all-reduce | flops 1024 | bytes 8192 | tf_op jit(solution)/shard_map/pmax | solution.py:19
  639.7 4.2 exponential_reduce_fusion
  643.9 12.4 %psum.55 = f32[1024]{0:T(1024)S(1)} all-reduce(f32[1024]{0:T(1024)S(1)} %exponential_reduce_fusion), channel_id=1, replica_groups=mesh['slot'=8,'asset'=32] {'slot'}, use_global_device_ids=true, to_apply=%region_25.0 | all-reduce | flops 1024 | bytes 8192 | tf_op jit(solution)/shard_map/psum | solution.py:20
  656.3 6.4 exponential_multiply_fusion
  (6 shorter events, 0.1 us)
Async XLA Ops:
  6.5 15.5 %copy-start.1 = (s32[1024]{0:T(1024)S(1)}, s32[1024]{0:T(1024)}, u32[]{:S(2)}) copy-start(s32[1024]{0:T(1024)} %param.7) | copy-start | bytes 12292
  9.5 83.4 %all-to-all-start = ((bf16[32,64,768]{2,1,0:T(8,128)(2,1)}), bf16[32,64,768]{2,1,0:T(8,128)(2,1)S(1)}, u32[]{:S(2)}, u32[]{:S(2)}) async-start(bf16[32,64,768]{2,1,0:T(8,128)(2,1)} %stack.2), calls=%async_computation | async-start | bytes 6291456 | tf_op jit(solution)/shard_map/all_to_all | solution.py:26
  21.3 31.7 %all-gather.2.cloned.1.call-start = ((), (), s32[]{:S(2)}) async-start(), calls=%async_computation.1 | async-start | bytes 1769472 | tf_op jit(solution)/shard_map/all_gather | solution.py:33
  100.0 124.5 %copy-start = (s32[2048]{0:T(1024)S(1)}, s32[2048]{0:T(1024)}, u32[]{:S(2)}) copy-start(s32[2048]{0:T(1024)} %param.6) | copy-start | bytes 24580
Sparse Core Ops, SparseCore 0:
  24.0 29.0 all-gather.1
